TPU v7x, 32 devices: a whole 2x2x4 slice. The times are simulated.
32 devices in a mesh: wide: 8 (over z, x), narrow: 4 (over y, core).
Axes of the slice: x: 2, y: 2, z: 4, core: 2. Of those that a mesh axis runs over, the one named last changes fastest.
Arguments:
- samples: bfloat16 [16384, 1024], P(('wide', 'narrow')), may hold values from -16 to 16
- centroid_table: bfloat16 [16384, 1024], P('wide', 'narrow'), may hold values from -6 to 6
- owner: int32 [16384], replicated, may hold values from 0 to 7, as said below
- slot: int32 [16384], replicated, may hold values from 0 to 2047, as said below
- assign: int32 [16384], P('wide'), may hold values from 0 to 16383, as said below
- codebook: float32 [8, 2048, 128], P('narrow'), may hold values from -16 to 16
Outputs:
- residual: bfloat16 [16384, 1024], P('wide', 'narrow')
- refined: float32 [8, 2048, 128], P('narrow')
Inputs may be any that keep to these rules, and one draw needn't show every extreme that they name: owner and slot give each coarse centroid a distinct storage position owner * 2048 + slot. `slot`: see owner. `assign`: in each aligned block of 2048 rows (the rows of one index of wide), at most 512 rows have centroids with one owner, and some owner has exactly 512.
All inputs are finite; a program needn't handle non-finite values.
Results may differ from a plain program's by a relative error of at most 0.0079.
Values may be sent and summed in bfloat16 or wider, within the bound.
No kernel may reach another device: no remote copies, remote signals or barrier semaphores. Data moves between devices by JAX's collectives and lax.ppermute only.
A program may use at most 64 MiB of HBM per device.

v0:
```python
import jax
import jax.numpy as jnp
from jax import lax
from jax.sharding import PartitionSpec as P

ITERS = 2
softness_level = 16.0
prior_weight = 1.0


def score_pass(blocks, narrow_words, codeword_norm_values):
    spaces = narrow_words.shape[0]
    words_count = narrow_words.shape[1]
    sub_width = narrow_words.shape[2]

    def block_step(running, row_block):
        inner_product_rows = jnp.einsum(
            "bms,mks->mbk", row_block, narrow_words, preferred_element_type=jnp.float32
        )
        score_matrix = (
            2.0 * inner_product_rows - codeword_norm_values[:, None, :]
        ) / softness_level
        weights_soft = jax.nn.softmax(score_matrix, axis=2).astype(jnp.bfloat16)
        totals = running[0] + jnp.einsum(
            "mbk,bms->mks", weights_soft, row_block, preferred_element_type=jnp.float32
        )
        return ((totals, running[1] + jnp.sum(weights_soft, axis=1, dtype=jnp.float32)), None)

    start = (
        jnp.zeros((spaces, words_count, sub_width), jnp.float32),
        jnp.zeros((spaces, words_count), jnp.float32),
    )
    (totals, counts), ignored = lax.scan(block_step, start, blocks)
    return (totals, counts)


def on_device(samples, centroid_table, owner, slot, assign, codebook):
    regrouped = lax.all_to_all(samples, "narrow", split_axis=1, concat_axis=0, tiled=True)
    group_rows = regrouped.shape[0]
    owner_of = owner[assign]
    slot_of = slot[assign]
    whole = lax.all_gather(centroid_table, "wide", axis=0, tiled=True)
    centre = jnp.take(whole, owner_of * centroid_table.shape[0] + slot_of, axis=0)
    residual = (regrouped.astype(jnp.float32) - centre.astype(jnp.float32)).astype(jnp.bfloat16)
    spaces = codebook.shape[0]
    sub_width = codebook.shape[2]
    block_size = 512
    blocks = residual.reshape(group_rows // block_size, block_size, spaces, sub_width)
    codewords = codebook
    narrow_words = codebook.astype(jnp.bfloat16)
    codeword_norm_values = jnp.sum(codebook * codebook, axis=2)
    for iteration in range(ITERS):
        narrow_words = codewords.astype(jnp.bfloat16)
        codeword_norm_values = jnp.sum(codewords * codewords, axis=2)
        totals, counts = score_pass(blocks, narrow_words, codeword_norm_values)
        totals, counts = lax.psum((totals, counts), "wide")
        codewords = (totals + prior_weight * codewords) / (counts[:, :, None] + prior_weight)
    return (residual, codewords)


def solution(mesh):
    return jax.shard_map(
        on_device,
        mesh=mesh,
        in_specs=(
            P(("wide", "narrow"), None),
            P("wide", "narrow"),
            P(),
            P(),
            P("wide"),
            P("narrow", None, None),
        ),
        out_specs=(P("wide", "narrow"), P("narrow", None, None)),
        check_vma=False,
    )
```

profile of v0, /device:TPU:0, one launch (start us, length us, event | category | flops | bytes accessed | tf_op | source)
XLA Modules:
  0.0 518.3 jit_solution(10853874548214603583)
XLA Ops:
  7.9 2.3 copy.14
  10.2 4.3 all-to-all-start
  14.5 11.8 %gather_fusion.1 = s32[2048]{0:T(1024)S(1)} fusion(s32[16384]{0:T(1024)S(1)} %copy-done, s32[2048]{0:T(1024)S(1)} %fusion.55), kind=kCustom, calls=%fused_computation.1 | custom fusion | bytes 24576 | tf_op jit(solution)/shard_map/gather | solution.py:41
  26.3 11.8 %gather_fusion = s32[2048]{0:T(1024)S(1)} fusion(s32[16384]{0:T(1024)S(1)} %copy-done.2, s32[2048]{0:T(1024)S(1)} %fusion.55), kind=kCustom, calls=%fused_computation | custom fusion | bytes 24576 | tf_op jit(solution)/shard_map/gather | solution.py:40
  38.2 3.9 multiply_reduce_fusion.1
  42.1 2.6 fusion.66
  44.7 92.6 %all-gather.2.cloned.1.call-done = bf16[16384,256]{1,0:T(8,128)(2,1)} async-done(((bf16[2048,256]{1,0:T(8,128)(2,1)}), bf16[16384,256]{1,0:T(8,128)(2,1)}) %all-gather.2.cloned.1.call-update) | async-done | bytes 8388624 | tf_op jit(solution)/shard_map/all_gather | solution.py:42
  137.4 11.1 %gather_fusion.2 = bf16[2048,256]{1,0:T(8,128)(2,1)S(1)} fusion(bf16[16384,256]{1,0:T(8,128)(2,1)} %all-gather.2.cloned.1.call-done, s32[2048]{0:T(1024)S(1)} %broadcast_clamp_fusion), kind=kCustom, calls=%fused_computation.2 | custom fusion | bytes 2105344 | tf_op jit(solution)/shard_map/jit(_take)/gather | solution.py:43
  148.5 1.4 gather.15
  149.8 3.7 copy.16
  153.5 3.3 subtract_convert_fusion
  156.8 1.6 copy.18
  158.4 69.5 %while.26 = (s32[]{:T(128)}, f32[2,2048,128]{2,1,0:T(8,128)S(1)}, f32[2,2048]{1,0:T(2,128)S(1)}, bf16[4,512,2,128]{3,1,2,0:T(8,128)(2,1)S(1)}, bf16[2,2048,128]{...) while((s32[]{:T(128)}, f32[2,2048,128]{2,1,0:T(8,128)S(1)}, ...), condition=%wide.region_5.6_spmd.clone, body=%wide.region_1.5_spmd.clone.sunk | while | flops 1093670912 | bytes 31023212 | solution.py:33
  158.4 7.2 %fusion.87 = (f32[2,512]{1,0:T(2,128)S(1)}, f32[2,512,2048]{2,1,0:T(8,128)}) fusion(f32[2,2048]{1,0:T(2,128)S(1)} %get-tuple-element.277, bf16[2,2048,128]{2,1,0:T(8,128)(2,1)} %get-tuple-element.276, bf16[4,512,2,128]{3,1,2,0:T(8,128)(2,1)S(1)} %get-tuple-element.275, s32[]{:T(128)S(6)} %copy.24), kind=kOutput, calls=%fused_computation.70.clone.1 | convolution fusion | flops 547358720 | bytes 9719812 | tf_op jit(solution)/shard_map/while/body/eval_jaxpr/sub | solution.py:23
  165.6 5.5 %convert_reduce_fusion.4 = (f32[2,2048]{1,0:T(2,128)S(1)}, bf16[2,512,2048]{2,1,0:T(8,128)(2,1)}) fusion(f32[2,512,2048]{2,1,0:T(8,128)} %get-tuple-element.242, f32[2,512]{1,0:T(2,128)S(1)} %get-tuple-element.243), kind=kLoop, calls=%fused_computation.4.clone.1 | loop fusion | flops 8384512 | bytes 12603392 | tf_op jit(solution)/shard_map/while/body/eval_jaxpr/reduce_sum | solution.py:27
  171.1 4.7 convolution_add_fusion.4
  175.8 7.2 %fusion.87 = (f32[2,512]{1,0:T(2,128)S(1)}, f32[2,512,2048]{2,1,0:T(8,128)}) fusion(f32[2,2048]{1,0:T(2,128)S(1)} %get-tuple-element.277, bf16[2,2048,128]{2,1,0:T(8,128)(2,1)} %get-tuple-element.276, bf16[4,512,2,128]{3,1,2,0:T(8,128)(2,1)S(1)} %get-tuple-element.275, s32[]{:T(128)S(6)} %copy.24), kind=kOutput, calls=%fused_computation.70.clone.1 | convolution fusion | flops 547358720 | bytes 9719812 | tf_op jit(solution)/shard_map/while/body/eval_jaxpr/sub | solution.py:23
  183.0 5.5 %convert_reduce_fusion.4 = (f32[2,2048]{1,0:T(2,128)S(1)}, bf16[2,512,2048]{2,1,0:T(8,128)(2,1)}) fusion(f32[2,512,2048]{2,1,0:T(8,128)} %get-tuple-element.242, f32[2,512]{1,0:T(2,128)S(1)} %get-tuple-element.243), kind=kLoop, calls=%fused_computation.4.clone.1 | loop fusion | flops 8384512 | bytes 12603392 | tf_op jit(solution)/shard_map/while/body/eval_jaxpr/reduce_sum | solution.py:27
  188.5 4.7 convolution_add_fusion.4
  193.2 7.2 %fusion.87 = (f32[2,512]{1,0:T(2,128)S(1)}, f32[2,512,2048]{2,1,0:T(8,128)}) fusion(f32[2,2048]{1,0:T(2,128)S(1)} %get-tuple-element.277, bf16[2,2048,128]{2,1,0:T(8,128)(2,1)} %get-tuple-element.276, bf16[4,512,2,128]{3,1,2,0:T(8,128)(2,1)S(1)} %get-tuple-element.275, s32[]{:T(128)S(6)} %copy.24), kind=kOutput, calls=%fused_computation.70.clone.1 | convolution fusion | flops 547358720 | bytes 9719812 | tf_op jit(solution)/shard_map/while/body/eval_jaxpr/sub | solution.py:23
  200.3 5.5 %convert_reduce_fusion.4 = (f32[2,2048]{1,0:T(2,128)S(1)}, bf16[2,512,2048]{2,1,0:T(8,128)(2,1)}) fusion(f32[2,512,2048]{2,1,0:T(8,128)} %get-tuple-element.242, f32[2,512]{1,0:T(2,128)S(1)} %get-tuple-element.243), kind=kLoop, calls=%fused_computation.4.clone.1 | loop fusion | flops 8384512 | bytes 12603392 | tf_op jit(solution)/shard_map/while/body/eval_jaxpr/reduce_sum | solution.py:27
  205.9 4.7 convolution_add_fusion.4
  210.6 7.2 %fusion.87 = (f32[2,512]{1,0:T(2,128)S(1)}, f32[2,512,2048]{2,1,0:T(8,128)}) fusion(f32[2,2048]{1,0:T(2,128)S(1)} %get-tuple-element.277, bf16[2,2048,128]{2,1,0:T(8,128)(2,1)} %get-tuple-element.276, bf16[4,512,2,128]{3,1,2,0:T(8,128)(2,1)S(1)} %get-tuple-element.275, s32[]{:T(128)S(6)} %copy.24), kind=kOutput, calls=%fused_computation.70.clone.1 | convolution fusion | flops 547358720 | bytes 9719812 | tf_op jit(solution)/shard_map/while/body/eval_jaxpr/sub | solution.py:23
  217.7 5.5 %convert_reduce_fusion.4 = (f32[2,2048]{1,0:T(2,128)S(1)}, bf16[2,512,2048]{2,1,0:T(8,128)(2,1)}) fusion(f32[2,512,2048]{2,1,0:T(8,128)} %get-tuple-element.242, f32[2,512]{1,0:T(2,128)S(1)} %get-tuple-element.243), kind=kLoop, calls=%fused_computation.4.clone.1 | loop fusion | flops 8384512 | bytes 12603392 | tf_op jit(solution)/shard_map/while/body/eval_jaxpr/reduce_sum | solution.py:27
  223.2 4.7 convolution_add_fusion.4
  228.0 1.3 copy-done.3
  229.4 35.4 %psum.29 = f32[2,2048]{1,0:T(2,128)S(1)} all-reduce(f32[2,2048]{1,0:T(2,128)S(1)} %get-tuple-element.69), channel_id=1, replica_groups=mesh['wide'=8,'narrow'=4] {'wide'}, use_global_device_ids=true, to_apply=%region_7.8 | all-reduce | flops 4096 | bytes 32768 | tf_op jit(solution)/shard_map/psum | solution.py:56
  264.8 65.7 %all-reduce.3.cloned.1.call-done = f32[2,2048,128]{2,1,0:T(8,128)} async-done(((f32[2,2048,128]{2,1,0:T(8,128)}), f32[2,2048,128]{2,1,0:T(8,128)}) %all-reduce.3.cloned.1.call-update) | async-done | bytes 2097168 | tf_op jit(solution)/shard_map/psum | solution.py:56
  330.5 2.9 multiply_reduce_fusion
  333.4 1.3 copy-done.5
  335.8 69.5 %while.27 = (s32[]{:T(128)}, f32[2,2048,128]{2,1,0:T(8,128)S(1)}, f32[2,2048]{1,0:T(2,128)S(1)}, bf16[4,512,2,128]{3,1,2,0:T(8,128)(2,1)S(1)}, bf16[2,2048,128]{...) while((s32[]{:T(128)}, f32[2,2048,128]{2,1,0:T(8,128)S(1)}, ...), condition=%wide.region_13.14_spmd.clone, body=%wide.region_9.0_spmd.clone.sunk | while | flops 1093670912 | bytes 31023212 | solution.py:33
  335.8 7.1 %fusion.92 = (f32[2,512]{1,0:T(2,128)S(1)}, f32[2,512,2048]{2,1,0:T(8,128)}) fusion(f32[2,2048]{1,0:T(2,128)S(1)} %get-tuple-element.301, bf16[2,2048,128]{2,1,0:T(8,128)(2,1)} %get-tuple-element.300, bf16[4,512,2,128]{3,1,2,0:T(8,128)(2,1)S(1)} %get-tuple-element.299, s32[]{:T(128)S(6)} %copy.34), kind=kOutput, calls=%fused_computation.71.clone.1 | convolution fusion | flops 547358720 | bytes 9719812 | tf_op jit(solution)/shard_map/while/body/eval_jaxpr/sub | solution.py:23
  342.9 5.5 %convert_reduce_fusion.5 = (f32[2,2048]{1,0:T(2,128)S(1)}, bf16[2,512,2048]{2,1,0:T(8,128)(2,1)}) fusion(f32[2,512,2048]{2,1,0:T(8,128)} %get-tuple-element.252, f32[2,512]{1,0:T(2,128)S(1)} %get-tuple-element.253), kind=kLoop, calls=%fused_computation.28.clone.1 | loop fusion | flops 8384512 | bytes 12603392 | tf_op jit(solution)/shard_map/while/body/eval_jaxpr/reduce_sum | solution.py:27
  348.4 4.7 convolution_add_fusion.5
  353.2 7.2 %fusion.92 = (f32[2,512]{1,0:T(2,128)S(1)}, f32[2,512,2048]{2,1,0:T(8,128)}) fusion(f32[2,2048]{1,0:T(2,128)S(1)} %get-tuple-element.301, bf16[2,2048,128]{2,1,0:T(8,128)(2,1)} %get-tuple-element.300, bf16[4,512,2,128]{3,1,2,0:T(8,128)(2,1)S(1)} %get-tuple-element.299, s32[]{:T(128)S(6)} %copy.34), kind=kOutput, calls=%fused_computation.71.clone.1 | convolution fusion | flops 547358720 | bytes 9719812 | tf_op jit(solution)/shard_map/while/body/eval_jaxpr/sub | solution.py:23
  360.3 5.5 %convert_reduce_fusion.5 = (f32[2,2048]{1,0:T(2,128)S(1)}, bf16[2,512,2048]{2,1,0:T(8,128)(2,1)}) fusion(f32[2,512,2048]{2,1,0:T(8,128)} %get-tuple-element.252, f32[2,512]{1,0:T(2,128)S(1)} %get-tuple-element.253), kind=kLoop, calls=%fused_computation.28.clone.1 | loop fusion | flops 8384512 | bytes 12603392 | tf_op jit(solution)/shard_map/while/body/eval_jaxpr/reduce_sum | solution.py:27
  365.8 4.7 convolution_add_fusion.5
  370.5 7.2 %fusion.92 = (f32[2,512]{1,0:T(2,128)S(1)}, f32[2,512,2048]{2,1,0:T(8,128)}) fusion(f32[2,2048]{1,0:T(2,128)S(1)} %get-tuple-element.301, bf16[2,2048,128]{2,1,0:T(8,128)(2,1)} %get-tuple-element.300, bf16[4,512,2,128]{3,1,2,0:T(8,128)(2,1)S(1)} %get-tuple-element.299, s32[]{:T(128)S(6)} %copy.34), kind=kOutput, calls=%fused_computation.71.clone.1 | convolution fusion | flops 547358720 | bytes 9719812 | tf_op jit(solution)/shard_map/while/body/eval_jaxpr/sub | solution.py:23
  377.7 5.5 %convert_reduce_fusion.5 = (f32[2,2048]{1,0:T(2,128)S(1)}, bf16[2,512,2048]{2,1,0:T(8,128)(2,1)}) fusion(f32[2,512,2048]{2,1,0:T(8,128)} %get-tuple-element.252, f32[2,512]{1,0:T(2,128)S(1)} %get-tuple-element.253), kind=kLoop, calls=%fused_computation.28.clone.1 | loop fusion | flops 8384512 | bytes 12603392 | tf_op jit(solution)/shard_map/while/body/eval_jaxpr/reduce_sum | solution.py:27
  383.2 4.7 convolution_add_fusion.5
  387.9 7.2 %fusion.92 = (f32[2,512]{1,0:T(2,128)S(1)}, f32[2,512,2048]{2,1,0:T(8,128)}) fusion(f32[2,2048]{1,0:T(2,128)S(1)} %get-tuple-element.301, bf16[2,2048,128]{2,1,0:T(8,128)(2,1)} %get-tuple-element.300, bf16[4,512,2,128]{3,1,2,0:T(8,128)(2,1)S(1)} %get-tuple-element.299, s32[]{:T(128)S(6)} %copy.34), kind=kOutput, calls=%fused_computation.71.clone.1 | convolution fusion | flops 547358720 | bytes 9719812 | tf_op jit(solution)/shard_map/while/body/eval_jaxpr/sub | solution.py:23
  395.1 5.5 %convert_reduce_fusion.5 = (f32[2,2048]{1,0:T(2,128)S(1)}, bf16[2,512,2048]{2,1,0:T(8,128)(2,1)}) fusion(f32[2,512,2048]{2,1,0:T(8,128)} %get-tuple-element.252, f32[2,512]{1,0:T(2,128)S(1)} %get-tuple-element.253), kind=kLoop, calls=%fused_computation.28.clone.1 | loop fusion | flops 8384512 | bytes 12603392 | tf_op jit(solution)/shard_map/while/body/eval_jaxpr/reduce_sum | solution.py:27
  400.6 4.7 convolution_add_fusion.5
  406.6 3.0 copy.15
  409.6 2.7 fusion.54
  412.3 36.7 %psum.31 = f32[2,2048]{1,0:T(2,128)S(1)} all-reduce(f32[2,2048]{1,0:T(2,128)S(1)} %get-tuple-element.71), channel_id=1, replica_groups=mesh['wide'=8,'narrow'=4] {'wide'}, use_global_device_ids=true, to_apply=%region_15.16 | all-reduce | flops 4096 | bytes 32768 | tf_op jit(solution)/shard_map/psum | solution.py:56
  449.0 59.9 %all-reduce.5.cloned.1.call-done = f32[2,2048,128]{2,1,0:T(8,128)} async-done(((f32[2,2048,128]{2,1,0:T(8,128)}), f32[2,2048,128]{2,1,0:T(8,128)}) %all-reduce.5.cloned.1.call-update) | async-done | bytes 2097168 | tf_op jit(solution)/shard_map/psum | solution.py:56
  508.9 2.9 add_divide_fusion
  (46 shorter events, 3.5 us)
Async XLA Ops:
  7.2 7.3 %copy-start = (s32[16384]{0:T(1024)S(1)}, s32[16384]{0:T(1024)}, u32[]{:S(2)}) copy-start(s32[16384]{0:T(1024)} %param.13) | copy-start | bytes 196612
  7.2 130.2 %all-gather.2.cloned.1.call-start = ((), (), s32[]{:S(2)}) async-start(), calls=%async_computation.1 | async-start | bytes 9437184 | tf_op jit(solution)/shard_map/all_gather | solution.py:42
  7.9 6.6 %copy-start.9 = (s32[2048]{0:T(1024)S(1)}, s32[2048]{0:T(1024)}, u32[]{:S(2)}) copy-start(s32[2048]{0:T(1024)} %param.14) | copy-start | bytes 24580
  10.2 31.9 %all-to-all-start = ((bf16[512,4,256]{0,2,1:T(8,128)(2,1)}), bf16[512,4,256]{0,2,1:T(8,128)(2,1)S(1)}, u32[]{:S(2)}, u32[]{:S(2)}) async-start(bf16[512,4,256]{0,2,1:T(8,128)(2,1)} %bitcast), calls=%async_computation | async-start | bytes 2097152 | tf_op jit(solution)/shard_map/all_to_all | solution.py:38
  14.5 316.0 %all-reduce.3.cloned.1.call-start = ((), (), s32[]{:S(2)}) async-start(), calls=%async_computation.2 | async-start | bytes 4194304 | tf_op jit(solution)/shard_map/psum | solution.py:56
  14.5 11.8 %copy-start.2 = (s32[16384]{0:T(1024)S(1)}, s32[16384]{0:T(1024)}, u32[]{:S(2)}) copy-start(s32[16384]{0:T(1024)} %param.12) | copy-start | bytes 196612
  148.5 5.1 copy-start.7
  227.9 1.3 copy-start.3
  229.3 279.6 %all-reduce.5.cloned.1.call-start = ((), (), s32[]{:S(2)}) async-start(), calls=%async_computation.3 | async-start | bytes 4194304 | tf_op jit(solution)/shard_map/psum | solution.py:56
  333.3 1.3 copy-start.5
  405.3 1.3 copy-start.4
  406.6 3.0 copy-start.8
  409.6 99.3 %copy-start.6 = (f32[2,2048,128]{2,1,0:T(8,128)S(1)}, f32[2,2048,128]{2,1,0:T(8,128)}, u32[]{:S(2)}) copy-start(f32[2,2048,128]{2,1,0:T(8,128)} %copy-done.5) | copy-start | bytes 6291460
  449.0 62.8 %copy-start.1 = (s32[16384]{0:T(1024)S(1)}, s32[16384]{0:T(1024)}, u32[]{:S(2)}) copy-start(s32[16384]{0:T(1024)} %param.13) | copy-start | bytes 196612
Sparse Core Ops, SparseCore 0:
  10.1 127.1 all-gather.1
  229.4 101.0 all-reduce.2
  406.7 102.1 all-reduce.4
where the time goes:
time: 519 us; the launch traced here: 518 us
  waiting for transfers between devices  219 us (42%)
  matrix products  94.6 us (18%)
  blocking collectives  72.1 us (14%)
  other arithmetic  63.7 us (12%)
  local copies, waits for them, and re-layouts  50.5 us (10%)
  between operations  14 us (3%)
    psum x2, waiting for transfers between devices, on_device(): totals, counts = lax.psum((totals, counts), 'wide')  126 us
    all_gather x1, waiting for transfers between devices, on_device(): whole = lax.all_gather(centroid_table, 'wide', axis=0, tiled=True)  92.6 us
    psum x2, blocking collectives, on_device(): totals, counts = lax.psum((totals, counts), 'wide')  72.1 us
    sub x8, matrix products, block_step(): weights_soft = jax.nn.softmax(score_matrix, axis=2).astype(jnp.bfloat16)  57.2 us
    reduce_sum x8, other arithmetic, block_step(): jnp.sum(weights_soft, axis=1, dtype=jnp.float32)  44.1 us
    dot_general x8, matrix products, block_step(): jnp.einsum('mbk,bms->mks', weights_soft, row_block, preferred_element_typ...  37.4 us
    gather x3, local copies, waits for them, and re-layouts, on_device(): jnp.take(whole, owner_of * centroid_table.shape[0] + slot_of, axis=0)  16.1 us
    gather x1, local copies, waits for them, and re-layouts, on_device(): slot_of = slot[assign]  11.8 us
  transfers between devices with their start and end apart: 4, of which 3 were waited for; matrix products, arithmetic and copies ran while one was open for 7% of the time, Pallas kernels for 0%

commit v1 on v0

--- a/solution.py
+++ b/solution.py
@@ -39,7 +39,31 @@
     group_rows = regrouped.shape[0]
     owner_of = owner[assign]
     slot_of = slot[assign]
-    whole = lax.all_gather(centroid_table, "wide", axis=0, tiled=True)
+
+    def make_records(vector):
+        res = lax.axis_size("wide")
+        reply, z, long_array = (res, lax.axis_index("wide"), vector.shape[0])
+        queue = tuple(((d, (d + 1) % reply) for d in range(reply)))
+        history = tuple(((d, (d - 1) % reply) for d in range(reply)))
+        x_next = jnp.zeros((*vector.shape[:0], reply * long_array, *vector.shape[1:]), vector.dtype)
+        x_next = lax.dynamic_update_slice_in_dim(x_next, vector, z * long_array, axis=0)
+        h_now = fresh = vector
+        current_block = reply // 2
+        jj = 1
+        while jj < current_block + 1:
+            h_now = lax.ppermute(h_now, axis_name="wide", perm=queue)
+            x_next = lax.dynamic_update_slice_in_dim(
+                x_next, h_now, (z - jj) % reply * long_array, axis=0
+            )
+            if jj < reply - current_block:
+                fresh = lax.ppermute(fresh, axis_name="wide", perm=history)
+                x_next = lax.dynamic_update_slice_in_dim(
+                    x_next, fresh, (z + jj) % reply * long_array, axis=0
+                )
+            jj += 1
+        return x_next
+
+    whole = make_records(centroid_table)
     centre = jnp.take(whole, owner_of * centroid_table.shape[0] + slot_of, axis=0)
     residual = (regrouped.astype(jnp.float32) - centre.astype(jnp.float32)).astype(jnp.bfloat16)
     spaces = codebook.shape[0]

time: 519 us -> 558 us (1.075)
  starting transfers between devices: 4.35 us -> 23.3 us
  local copies, waits for them, and re-layouts: 50.5 us -> 68.8 us
    ppermute x0 -> x7, waiting for transfers between devices: none -> 93.8 us  [the longest x4 93.8 us: make_records(): h_now = lax.ppermute(h_now, axis_name='wide', perm=queue)]
    all_gather x1 -> x0, waiting for transfers between devices: 92.6 us -> none  [on_device(): whole = lax.all_gather(centroid_table, 'wide', axis=0, tiled=True)]
    ppermute x0 -> x7, starting transfers between devices: none -> 19.7 us  [the longest x4 10.5 us: make_records(): h_now = lax.ppermute(h_now, axis_name='wide', perm=queue)]
    dynamic_update_slice x0 -> x8, local copies, waits for them, and re-layouts: none -> 14.6 us  [the longest x4 7.91 us: make_records(): lax.dynamic_update_slice_in_dim(x_next, h_now, (z - jj) % reply * long_ar...]
  transfers between devices with their start and end apart: 4 -> 10, of which waited for: 3 -> 6; matrix products, arithmetic and copies ran while one was open for 7% -> 10% of each run, Pallas kernels for 0% -> 0%
where the time goes in v1:
time: 558 us; the launch traced here: 557 us
  waiting for transfers between devices  219 us (39%)
  matrix products  94.6 us (17%)
  blocking collectives  72.5 us (13%)
  local copies, waits for them, and re-layouts  68.8 us (12%)
  other arithmetic  64.6 us (12%)
  starting transfers between devices  23.3 us (4%)
  between operations  14.2 us (3%)
    psum x2, waiting for transfers between devices, on_device(): totals, counts = lax.psum((totals, counts), 'wide')  125 us
    ppermute x4, waiting for transfers between devices, make_records(): h_now = lax.ppermute(h_now, axis_name='wide', perm=queue)  93.8 us
    psum x2, blocking collectives, on_device(): totals, counts = lax.psum((totals, counts), 'wide')  72.5 us
    sub x8, matrix products, block_step(): weights_soft = jax.nn.softmax(score_matrix, axis=2).astype(jnp.bfloat16)  57.2 us
    reduce_sum x8, other arithmetic, block_step(): jnp.sum(weights_soft, axis=1, dtype=jnp.float32)  44.1 us
    dot_general x8, matrix products, block_step(): jnp.einsum('mbk,bms->mks', weights_soft, row_block, preferred_element_typ...  37.4 us
    gather x3, local copies, waits for them, and re-layouts, on_device(): jnp.take(whole, owner_of * centroid_table.shape[0] + slot_of, axis=0)  16.1 us
    gather x1, local copies, waits for them, and re-layouts, on_device(): slot_of = slot[assign]  11.8 us
  transfers between devices with their start and end apart: 10, of which 6 were waited for; matrix products, arithmetic and copies ran while one was open for 10% of the time, Pallas kernels for 0%

profile of v1, /device:TPU:0, one launch (start us, length us, event | category | flops | bytes accessed | tf_op | source)
XLA Modules:
  0.0 557.2 jit_solution(17498703096979642968)
XLA Ops:
  7.2 3.0 collective-permute-start
  10.2 3.1 collective-permute-start.1
  15.6 3.5 all-to-all-start
  19.9 11.8 %gather_fusion = s32[2048]{0:T(1024)S(1)} fusion(s32[16384]{0:T(1024)S(1)} %copy-done, s32[2048]{0:T(1024)S(1)} %fusion.55), kind=kCustom, calls=%fused_computation | custom fusion | bytes 24576 | tf_op jit(solution)/shard_map/gather | solution.py:40
  31.7 11.8 %gather_fusion.1 = s32[2048]{0:T(1024)S(1)} fusion(s32[16384]{0:T(1024)S(1)} %copy-done.2, s32[2048]{0:T(1024)S(1)} %fusion.55), kind=kCustom, calls=%fused_computation.1 | custom fusion | bytes 24576 | tf_op jit(solution)/shard_map/gather | solution.py:41
  43.5 11.9 %collective-permute-done = bf16[2048,256]{1,0:T(8,128)(2,1)} collective-permute-done((bf16[2048,256]{1,0:T(8,128)(2,1)}, bf16[2048,256]{1,0:T(8,128)(2,1)}, u32[]{:S(2)}, u32[]{:S(2)}) %collective-permute-start) | collective-permute-done | bytes 1048608 | tf_op jit(solution)/shard_map/ppermute | solution.py:54
  57.9 3.6 broadcast_in_dim.31
  62.6 3.1 collective-permute-start.3
  65.7 36.6 %collective-permute-done.2 = bf16[2048,256]{1,0:T(8,128)(2,1)} collective-permute-done((bf16[2048,256]{1,0:T(8,128)(2,1)}, bf16[2048,256]{1,0:T(8,128)(2,1)}, u32[]{:S(2)}, u32[]{:S(2)}) %collective-permute-start.2) | collective-permute-done | bytes 1048608 | tf_op jit(solution)/shard_map/ppermute | solution.py:54
  104.7 3.9 multiply_reduce_fusion.1
  111.2 3.0 collective-permute-start.5
  116.6 31.7 %collective-permute-done.4 = bf16[2048,256]{1,0:T(8,128)(2,1)} collective-permute-done((bf16[2048,256]{1,0:T(8,128)(2,1)}, bf16[2048,256]{1,0:T(8,128)(2,1)}, u32[]{:S(2)}, u32[]{:S(2)}) %collective-permute-start.4) | collective-permute-done | bytes 1048608 | tf_op jit(solution)/shard_map/ppermute | solution.py:54
  161.0 13.6 %collective-permute-done.6 = bf16[2048,256]{1,0:T(8,128)(2,1)S(1)} collective-permute-done((bf16[2048,256]{1,0:T(8,128)(2,1)}, bf16[2048,256]{1,0:T(8,128)(2,1)S(1)}, u32[]{:S(2)}, u32[]{:S(2)}) %collective-permute-start.6) | collective-permute-done | bytes 1048608 | tf_op jit(solution)/shard_map/ppermute | solution.py:54
  175.6 11.1 %gather_fusion.2 = bf16[2048,256]{1,0:T(8,128)(2,1)S(1)} fusion(bf16[16384,256]{1,0:T(8,128)(2,1)} %constant_dynamic-update-slice_fusion, s32[2048]{0:T(1024)S(1)} %broadcast_clamp_fusion), kind=kCustom, calls=%fused_computation.2 | custom fusion | bytes 2105344 | tf_op jit(solution)/shard_map/jit(_take)/gather | solution.py:67
  188.1 3.7 copy.16
  191.7 3.3 subtract_convert_fusion
  196.6 69.5 %while.26 = (s32[]{:T(128)}, f32[2,2048,128]{2,1,0:T(8,128)S(1)}, f32[2,2048]{1,0:T(2,128)S(1)}, bf16[4,512,2,128]{3,1,2,0:T(8,128)(2,1)S(1)}, bf16[2,2048,128]{...) while((s32[]{:T(128)}, f32[2,2048,128]{2,1,0:T(8,128)S(1)}, ...), condition=%wide.region_5.6_spmd.clone, body=%wide.region_1.5_spmd.clone.sunk | while | flops 1093670912 | bytes 31023204 | solution.py:33
  196.7 7.2 %fusion.87 = (f32[2,512]{1,0:T(2,128)S(1)}, f32[2,512,2048]{2,1,0:T(8,128)}) fusion(f32[2,2048]{1,0:T(2,128)S(1)} %get-tuple-element.277, bf16[2,2048,128]{2,1,0:T(8,128)(2,1)} %get-tuple-element.276, bf16[4,512,2,128]{3,1,2,0:T(8,128)(2,1)S(1)} %get-tuple-element.275, s32[]{:T(128)} %get-tuple-element.264), kind=kOutput, calls=%fused_computation.78.clone.1 | convolution fusion | flops 547358720 | bytes 9719812 | tf_op jit(solution)/shard_map/while/body/eval_jaxpr/sub | solution.py:23
  203.8 5.5 convert_reduce_fusion.4
  209.3 4.7 convolution_add_fusion.4
  214.0 7.2 %fusion.87 = (f32[2,512]{1,0:T(2,128)S(1)}, f32[2,512,2048]{2,1,0:T(8,128)}) fusion(f32[2,2048]{1,0:T(2,128)S(1)} %get-tuple-element.277, bf16[2,2048,128]{2,1,0:T(8,128)(2,1)} %get-tuple-element.276, bf16[4,512,2,128]{3,1,2,0:T(8,128)(2,1)S(1)} %get-tuple-element.275, s32[]{:T(128)} %get-tuple-element.264), kind=kOutput, calls=%fused_computation.78.clone.1 | convolution fusion | flops 547358720 | bytes 9719812 | tf_op jit(solution)/shard_map/while/body/eval_jaxpr/sub | solution.py:23
  221.2 5.5 convert_reduce_fusion.4
  226.7 4.7 convolution_add_fusion.4
  231.4 7.2 %fusion.87 = (f32[2,512]{1,0:T(2,128)S(1)}, f32[2,512,2048]{2,1,0:T(8,128)}) fusion(f32[2,2048]{1,0:T(2,128)S(1)} %get-tuple-element.277, bf16[2,2048,128]{2,1,0:T(8,128)(2,1)} %get-tuple-element.276, bf16[4,512,2,128]{3,1,2,0:T(8,128)(2,1)S(1)} %get-tuple-element.275, s32[]{:T(128)} %get-tuple-element.264), kind=kOutput, calls=%fused_computation.78.clone.1 | convolution fusion | flops 547358720 | bytes 9719812 | tf_op jit(solution)/shard_map/while/body/eval_jaxpr/sub | solution.py:23
  238.6 5.5 convert_reduce_fusion.4
  244.1 4.7 convolution_add_fusion.4
  248.8 7.2 %fusion.87 = (f32[2,512]{1,0:T(2,128)S(1)}, f32[2,512,2048]{2,1,0:T(8,128)}) fusion(f32[2,2048]{1,0:T(2,128)S(1)} %get-tuple-element.277, bf16[2,2048,128]{2,1,0:T(8,128)(2,1)} %get-tuple-element.276, bf16[4,512,2,128]{3,1,2,0:T(8,128)(2,1)S(1)} %get-tuple-element.275, s32[]{:T(128)} %get-tuple-element.264), kind=kOutput, calls=%fused_computation.78.clone.1 | convolution fusion | flops 547358720 | bytes 9719812 | tf_op jit(solution)/shard_map/while/body/eval_jaxpr/sub | solution.py:23
  256.0 5.5 convert_reduce_fusion.4
  261.5 4.7 convolution_add_fusion.4
  267.6 36.0 %psum.29 = f32[2,2048]{1,0:T(2,128)S(1)} all-reduce(f32[2,2048]{1,0:T(2,128)S(1)} %get-tuple-element.69), channel_id=1, replica_groups=mesh['wide'=8,'narrow'=4] {'wide'}, use_global_device_ids=true, to_apply=%region_7.8 | all-reduce | flops 4096 | bytes 32768 | tf_op jit(solution)/shard_map/psum | solution.py:80
  303.6 65.3 %all-reduce.3.cloned.1.call-done = f32[2,2048,128]{2,1,0:T(8,128)} async-done(((f32[2,2048,128]{2,1,0:T(8,128)}), f32[2,2048,128]{2,1,0:T(8,128)}) %all-reduce.3.cloned.1.call-update) | async-done | bytes 2097168 | tf_op jit(solution)/shard_map/psum | solution.py:80
  374.3 69.5 %while.27 = (s32[]{:T(128)}, f32[2,2048,128]{2,1,0:T(8,128)S(1)}, f32[2,2048]{1,0:T(2,128)S(1)}, bf16[4,512,2,128]{3,1,2,0:T(8,128)(2,1)S(1)}, bf16[2,2048,128]{...) while((s32[]{:T(128)}, f32[2,2048,128]{2,1,0:T(8,128)S(1)}, ...), condition=%wide.region_13.14_spmd.clone, body=%wide.region_9.13_spmd.clone.sunk | while | flops 1093670912 | bytes 31023204 | solution.py:33
  374.3 7.1 %fusion.92 = (f32[2,512]{1,0:T(2,128)S(1)}, f32[2,512,2048]{2,1,0:T(8,128)}) fusion(f32[2,2048]{1,0:T(2,128)S(1)} %get-tuple-element.301, bf16[2,2048,128]{2,1,0:T(8,128)(2,1)} %get-tuple-element.300, bf16[4,512,2,128]{3,1,2,0:T(8,128)(2,1)S(1)} %get-tuple-element.299, s32[]{:T(128)} %get-tuple-element.288), kind=kOutput, calls=%fused_computation.79.clone.1 | convolution fusion | flops 547358720 | bytes 9719812 | tf_op jit(solution)/shard_map/while/body/eval_jaxpr/sub | solution.py:23
  381.4 5.5 convert_reduce_fusion.5
  386.9 4.7 convolution_add_fusion.5
  391.6 7.2 %fusion.92 = (f32[2,512]{1,0:T(2,128)S(1)}, f32[2,512,2048]{2,1,0:T(8,128)}) fusion(f32[2,2048]{1,0:T(2,128)S(1)} %get-tuple-element.301, bf16[2,2048,128]{2,1,0:T(8,128)(2,1)} %get-tuple-element.300, bf16[4,512,2,128]{3,1,2,0:T(8,128)(2,1)S(1)} %get-tuple-element.299, s32[]{:T(128)} %get-tuple-element.288), kind=kOutput, calls=%fused_computation.79.clone.1 | convolution fusion | flops 547358720 | bytes 9719812 | tf_op jit(solution)/shard_map/while/body/eval_jaxpr/sub | solution.py:23
  398.8 5.5 convert_reduce_fusion.5
  404.3 4.7 convolution_add_fusion.5
  409.0 7.2 %fusion.92 = (f32[2,512]{1,0:T(2,128)S(1)}, f32[2,512,2048]{2,1,0:T(8,128)}) fusion(f32[2,2048]{1,0:T(2,128)S(1)} %get-tuple-element.301, bf16[2,2048,128]{2,1,0:T(8,128)(2,1)} %get-tuple-element.300, bf16[4,512,2,128]{3,1,2,0:T(8,128)(2,1)S(1)} %get-tuple-element.299, s32[]{:T(128)} %get-tuple-element.288), kind=kOutput, calls=%fused_computation.79.clone.1 | convolution fusion | flops 547358720 | bytes 9719812 | tf_op jit(solution)/shard_map/while/body/eval_jaxpr/sub | solution.py:23
  416.2 5.5 convert_reduce_fusion.5
  421.7 4.7 convolution_add_fusion.5
  426.4 7.2 %fusion.92 = (f32[2,512]{1,0:T(2,128)S(1)}, f32[2,512,2048]{2,1,0:T(8,128)}) fusion(f32[2,2048]{1,0:T(2,128)S(1)} %get-tuple-element.301, bf16[2,2048,128]{2,1,0:T(8,128)(2,1)} %get-tuple-element.300, bf16[4,512,2,128]{3,1,2,0:T(8,128)(2,1)S(1)} %get-tuple-element.299, s32[]{:T(128)} %get-tuple-element.288), kind=kOutput, calls=%fused_computation.79.clone.1 | convolution fusion | flops 547358720 | bytes 9719812 | tf_op jit(solution)/shard_map/while/body/eval_jaxpr/sub | solution.py:23
  433.5 5.5 convert_reduce_fusion.5
  439.1 4.7 convolution_add_fusion.5
  445.1 3.0 copy.15
  448.1 2.9 fusion.54
  451.1 36.5 %psum.31 = f32[2,2048]{1,0:T(2,128)S(1)} all-reduce(f32[2,2048]{1,0:T(2,128)S(1)} %get-tuple-element.71), channel_id=1, replica_groups=mesh['wide'=8,'narrow'=4] {'wide'}, use_global_device_ids=true, to_apply=%region_15.16 | all-reduce | flops 4096 | bytes 32768 | tf_op jit(solution)/shard_map/psum | solution.py:80
  487.5 59.9 %all-reduce.5.cloned.1.call-done = f32[2,2048,128]{2,1,0:T(8,128)} async-done(((f32[2,2048,128]{2,1,0:T(8,128)}), f32[2,2048,128]{2,1,0:T(8,128)}) %all-reduce.5.cloned.1.call-update) | async-done | bytes 2097168 | tf_op jit(solution)/shard_map/psum | solution.py:80
  (64 shorter events, 41.8 us)
Async XLA Ops:
  7.2 12.7 %copy-start = (s32[16384]{0:T(1024)S(1)}, s32[16384]{0:T(1024)}, u32[]{:S(2)}) copy-start(s32[16384]{0:T(1024)} %param.12) | copy-start | bytes 196612
  7.2 24.5 %copy-start.2 = (s32[16384]{0:T(1024)S(1)}, s32[16384]{0:T(1024)}, u32[]{:S(2)}) copy-start(s32[16384]{0:T(1024)} %param.13) | copy-start | bytes 196612
  7.2 48.2 %collective-permute-start = (bf16[2048,256]{1,0:T(8,128)(2,1)}, bf16[2048,256]{1,0:T(8,128)(2,1)}, u32[]{:S(2)}, u32[]{:S(2)}) collective-permute-start(bf16[2048,256]{1,0:T(8,128)(2,1)} %param.11), channel_id=1, source_target_pairs={{0,4},{4,8},{8,12},{12,16},{16,20},{20,24},{24,28},{28,0},{1,5},{5... | collective-permute-start | bytes 3145736 | tf_op jit(solution)/shard_map/ppermute | solution.py:54
  10.2 52.4 %collective-permute-start.1 = (bf16[2048,256]{1,0:T(8,128)(2,1)}, bf16[2048,256]{1,0:T(8,128)(2,1)}, u32[]{:S(2)}, u32[]{:S(2)}) collective-permute-start(bf16[2048,256]{1,0:T(8,128)(2,1)} %param.11), channel_id=1, source_target_pairs={{0,28},{4,0},{8,4},{12,8},{16,12},{20,16},{24,20},{28,24},{1,29},{... | collective-permute-start | bytes 3145736 | tf_op jit(solution)/shard_map/ppermute | solution.py:59
  15.6 93.0 %all-to-all-start = ((bf16[512,4,256]{0,2,1:T(8,128)(2,1)}), bf16[512,4,256]{0,2,1:T(8,128)(2,1)S(1)}, u32[]{:S(2)}, u32[]{:S(2)}) async-start(bf16[512,4,256]{0,2,1:T(8,128)(2,1)} %bitcast), calls=%async_computation | async-start | bytes 2097152 | tf_op jit(solution)/shard_map/all_to_all | solution.py:38
  19.1 349.8 %all-reduce.3.cloned.1.call-start = ((), (), s32[]{:S(2)}) async-start(), calls=%async_computation.1 | async-start | bytes 4194304 | tf_op jit(solution)/shard_map/psum | solution.py:80
  31.7 29.8 %copy-start.8 = (bf16[2048,256]{1,0:T(8,128)(2,1)S(1)}, bf16[2048,256]{1,0:T(8,128)(2,1)}, u32[]{:S(2)}) copy-start(bf16[2048,256]{1,0:T(8,128)(2,1)} %param.11) | copy-start | bytes 3145732
  55.4 46.8 %collective-permute-start.2 = (bf16[2048,256]{1,0:T(8,128)(2,1)}, bf16[2048,256]{1,0:T(8,128)(2,1)}, u32[]{:S(2)}, u32[]{:S(2)}) collective-permute-start(bf16[2048,256]{1,0:T(8,128)(2,1)} %collective-permute-done), channel_id=1, source_target_pairs={{0,4},{4,8},{8,12},{12,16},{16,20},{20,24},{24,28},{28,0},{1,5},{5... | collective-permute-start | bytes 3145736 | tf_op jit(solution)/shard_map/ppermute | solution.py:54
  62.6 48.7 %collective-permute-start.3 = (bf16[2048,256]{1,0:T(8,128)(2,1)}, bf16[2048,256]{1,0:T(8,128)(2,1)}, u32[]{:S(2)}, u32[]{:S(2)}) collective-permute-start(bf16[2048,256]{1,0:T(8,128)(2,1)} %collective-permute-done.1), channel_id=1, source_target_pairs={{0,28},{4,0},{8,4},{12,8},{16,12},{20,16},{24,20},{28,24},{1,29},{... | collective-permute-start | bytes 3145736 | tf_op jit(solution)/shard_map/ppermute | solution.py:59
  102.2 46.0 %collective-permute-start.4 = (bf16[2048,256]{1,0:T(8,128)(2,1)}, bf16[2048,256]{1,0:T(8,128)(2,1)}, u32[]{:S(2)}, u32[]{:S(2)}) collective-permute-start(bf16[2048,256]{1,0:T(8,128)(2,1)} %collective-permute-done.2), channel_id=1, source_target_pairs={{0,4},{4,8},{8,12},{12,16},{16,20},{20,24},{24,28},{28,0},{1,5},{5... | collective-permute-start | bytes 3145736 | tf_op jit(solution)/shard_map/ppermute | solution.py:54
  111.2 48.7 %collective-permute-start.5 = (bf16[2048,256]{1,0:T(8,128)(2,1)}, bf16[2048,256]{1,0:T(8,128)(2,1)S(1)}, u32[]{:S(2)}, u32[]{:S(2)}) collective-permute-start(bf16[2048,256]{1,0:T(8,128)(2,1)} %collective-permute-done.3), channel_id=1, source_target_pairs={{0,28},{4,0},{8,4},{12,8},{16,12},{20,16},{24,20},{28,24},{1,29},{... | collective-permute-start | bytes 3145736 | tf_op jit(solution)/shard_map/ppermute | solution.py:59
  148.2 26.3 %collective-permute-start.6 = (bf16[2048,256]{1,0:T(8,128)(2,1)}, bf16[2048,256]{1,0:T(8,128)(2,1)S(1)}, u32[]{:S(2)}, u32[]{:S(2)}) collective-permute-start(bf16[2048,256]{1,0:T(8,128)(2,1)} %collective-permute-done.4), channel_id=1, source_target_pairs={{0,4},{4,8},{8,12},{12,16},{16,20},{20,24},{24,28},{28,0},{1,5},{5... | collective-permute-start | bytes 3145736 | tf_op jit(solution)/shard_map/ppermute | solution.py:54
  186.7 5.1 copy-start.7
  266.2 1.3 copy-start.3
  267.5 279.9 %all-reduce.5.cloned.1.call-start = ((), (), s32[]{:S(2)}) async-start(), calls=%async_computation.2 | async-start | bytes 4194304 | tf_op jit(solution)/shard_map/psum | solution.py:80
  371.8 1.3 copy-start.5
  443.8 1.3 copy-start.4
  443.8 106.5 %copy-start.1 = (s32[16384]{0:T(1024)S(1)}, s32[16384]{0:T(1024)}, u32[]{:S(2)}) copy-start(s32[16384]{0:T(1024)} %param.12) | copy-start | bytes 196612
  445.1 102.3 %copy-start.6 = (f32[2,2048,128]{2,1,0:T(8,128)S(1)}, f32[2,2048,128]{2,1,0:T(8,128)}, u32[]{:S(2)}) copy-start(f32[2,2048,128]{2,1,0:T(8,128)} %copy-done.5) | copy-start | bytes 6291460
Sparse Core Ops, SparseCore 0:
  267.6 101.2 all-reduce.2
  445.2 102.1 all-reduce.4
